TPU v7x, 128 devices: a whole 4x4x4 slice. The times are simulated.
128 devices in a mesh: lat: 8 (over x, y_hi), lon: 16 (over z, y_lo, core).
Axes of the slice: x: 4, y: 4 (y_hi: 2, y_lo: 2; y = y_hi * 2 + y_lo), z: 4, core: 2. Of those that a mesh axis runs over, the one named last changes fastest.
Arguments:
- features: bfloat16 [256, 384, 2048], P('lat', 'lon'), may hold values from -6 to 6
- atrous_weight: bfloat16 [3, 3, 2048, 256], replicated, may hold values from -0.046875 to 0.046875
- norm_gain: float32 [256], replicated, may hold values from 0.1 to 1.9
- norm_bias: float32 [256], replicated, may hold values from -0.5 to 0.5
- head_weight: float32 [3, 256], replicated, may hold values from -1.5 to 1.5
- labels: int32 [256, 384], P('lat', 'lon'), may hold values from 0 to 2
Outputs:
- mean_loss: float32 [], replicated
- grad_features: bfloat16 [256, 384, 2048], P('lat', 'lon')
- grad_weight: float32 [2048, 3, 3, 256], P('lat', None, None, 'lon')
- grad_gain: float32 [256], replicated
- grad_bias: float32 [256], replicated
- grad_head: float32 [3, 256], replicated
All inputs are finite; a program needn't handle non-finite values.
Results may differ from a plain program's by a relative error of at most 0.022.
Values may be sent and summed in bfloat16 or wider, within the bound.
No kernel may reach another device: no remote copies, remote signals or barrier semaphores. Data moves between devices by JAX's collectives and lax.ppermute only.
A program may use at most 192 MiB of HBM per device.

v0:
```python
import jax
import jax.numpy as jnp
from jax import lax
from jax.sharding import PartitionSpec as P

RATE = 12
epsilon = 1e-05


def padded_2(block, sides, width, periodic):
    for axis, dim in sides:
        count = lax.axis_size(axis)
        forward = [(i, i + 1) for i in range(count - 1)]
        if periodic:
            forward.append((count - 1, 0))
        backward = [(target, source) for source, target in forward]
        low = lax.ppermute(
            lax.slice_in_dim(block, block.shape[dim] - width, None, axis=dim), axis, forward
        )
        high = lax.ppermute(lax.slice_in_dim(block, 0, width, axis=dim), axis, backward)
        block = jnp.concatenate([low, block, high], axis=dim)
    return block


def shards(features, atrous_weight, norm_gain, norm_bias, head_weight, labels):
    height, breadth, channels = features.shape
    filters = atrous_weight.shape[3]
    local_cells = height * breadth
    total_cells = local_cells * lax.axis_size("lat") * lax.axis_size("lon")
    flat_input = features.reshape(local_cells, channels)
    lon_padded = padded_2(features, (("lon", 1),), RATE, True)
    padded = padded_2(lon_padded, (("lat", 0),), RATE, False)
    summed = jnp.zeros((local_cells, filters), jnp.float32)
    for tap_row in range(3):
        for tap_col in range(3):
            window = padded[
                tap_row * RATE : tap_row * RATE + height, tap_col * RATE : tap_col * RATE + breadth
            ]
            summed = summed + jnp.dot(
                window.reshape(local_cells, channels),
                atrous_weight[tap_row, tap_col],
                preferred_element_type=jnp.float32,
            )
    moments = lax.psum((jnp.sum(summed, 0), jnp.sum(summed * summed, 0)), ("lat", "lon"))
    average = moments[0] / total_cells
    variance = moments[1] / total_cells - average * average
    inverse = lax.rsqrt(variance + epsilon)
    normed = (summed - average) * inverse
    preact = norm_gain * normed + norm_bias
    hidden = jnp.maximum(preact, 0.0).astype(jnp.bfloat16)
    hidden_wide = hidden.astype(jnp.float32)
    logits = jnp.dot(hidden_wide, head_weight.T, precision=lax.Precision.HIGHEST)
    one_hot = (
        labels.reshape(local_cells)[:, None]
        == jnp.arange(head_weight.shape[0], dtype=jnp.int32)[None, :]
    ).astype(jnp.float32)
    exponent = jnp.exp(logits)
    partition = jnp.sum(exponent, 1, keepdims=True)
    loss_terms = jnp.sum(jnp.log(partition)[:, 0] - jnp.sum(logits * one_hot, 1))
    grad_logits = exponent / partition - one_hot
    head_term = jnp.dot(grad_logits.T, hidden_wide, precision=lax.Precision.HIGHEST)
    d_hidden = jnp.dot(grad_logits, head_weight, precision=lax.Precision.HIGHEST)
    d_preact = jnp.where(preact > 0, d_hidden, 0.0)
    totals = lax.psum(
        (jnp.sum(d_preact, 0), jnp.sum(d_preact * normed, 0), head_term, loss_terms), ("lat", "lon")
    )
    grad_bias = totals[0] / total_cells
    grad_gain = totals[1] / total_cells
    grad_head = totals[2] / total_cells
    mean_loss = totals[3] / total_cells
    d_summed = (norm_gain * inverse * (d_preact - grad_bias - normed * grad_gain)).astype(
        jnp.bfloat16
    )
    d_grid = d_summed.reshape(height, breadth, filters)
    grad_lon = padded_2(d_grid, (("lon", 1),), RATE, True)
    grad_padded = padded_2(grad_lon, (("lat", 0),), RATE, False)
    grad_acc = jnp.zeros((local_cells, channels), jnp.float32)
    shifted_taps = []
    for tap_row in range(3):
        for tap_col in range(3):
            row_first = (2 - tap_row) * RATE
            col_first = (2 - tap_col) * RATE
            shifted = grad_padded[
                row_first : row_first + height, col_first : col_first + breadth
            ].reshape(local_cells, filters)
            shifted_taps.append(shifted)
            grad_acc = grad_acc + lax.dot_general(
                shifted,
                atrous_weight[tap_row, tap_col],
                (((1,), (1,)), ((), ())),
                preferred_element_type=jnp.float32,
            )
    grad_features = grad_acc.astype(jnp.bfloat16).reshape(height, breadth, channels)
    channel_block = channels // lax.axis_size("lat")
    filter_block = filters // lax.axis_size("lon")
    shifted_all = jnp.stack(shifted_taps, 0)
    lon_summed = lax.psum_scatter(
        jnp.einsum(
            "tqf,qc->ftc", shifted_all, flat_input, preferred_element_type=jnp.float32
        ).astype(jnp.bfloat16),
        "lon",
        scatter_dimension=0,
        tiled=True,
    )
    weight_block = jnp.transpose(
        lax.psum_scatter(lon_summed, "lat", scatter_dimension=2, tiled=True).astype(jnp.float32),
        (2, 1, 0),
    )
    grad_weight = (weight_block / total_cells).reshape(channel_block, 3, 3, filter_block)
    return (mean_loss, grad_features, grad_weight, grad_gain, grad_bias, grad_head)


def solution(mesh):
    return jax.shard_map(
        shards,
        mesh=mesh,
        in_specs=(P("lat", "lon", None), P(), P(), P(), P(), P("lat", "lon")),
        out_specs=(P(), P("lat", "lon", None), P("lat", None, None, "lon"), P(), P(), P()),
        check_vma=False,
    )
```

profile of v0, /device:TPU:0, one launch (start us, length us, event | category | flops | bytes accessed | tf_op | source)
XLA Modules:
  0.0 566.8 jit_solution(16156541013725347236)
XLA Ops:
  7.2 3.1 fusion.63
  11.2 4.6 collective-permute-start.1
  16.8 31.3 %collective-permute-done.1 = bf16[32,12,2048]{2,0,1:T(8,128)(2,1)S(1)} collective-permute-done((bf16[32,12,2048]{2,0,1:T(8,128)(2,1)S(1)}, bf16[32,12,2048]{2,0,1:T(8,128)(2,1)S(1)}, u32[]{:S(2)}, u32[]{:S(2)}) %collective-permute-start.1) | collective-permute-done | bytes 1572896 | tf_op jit(solution)/shard_map/ppermute | solution.py:20
  52.6 4.8 pad_maximum_fusion.5
  57.4 6.4 %collective-permute-start.2 = (bf16[12,48,2048]{2,1,0:T(8,128)(2,1)}, bf16[12,48,2048]{2,1,0:T(8,128)(2,1)}, u32[]{:S(2)}, u32[]{:S(2)}) collective-permute-start(bf16[12,48,2048]{2,1,0:T(8,128)(2,1)} %get-tuple-element.26), channel_id=1, source_target_pairs={{0,16},{16,32},{32,48},{48,64},{64,80},{80,96},{96,112},{1,17},{17... | collective-permute-start | bytes 7077896 | tf_op jit(solution)/shard_map/ppermute | solution.py:17
  67.9 4.2 pad_maximum_fusion.1
  72.0 3.1 fusion.26
  75.1 83.8 %collective-permute-done.2 = bf16[12,48,2048]{2,1,0:T(8,128)(2,1)} collective-permute-done((bf16[12,48,2048]{2,1,0:T(8,128)(2,1)}, bf16[12,48,2048]{2,1,0:T(8,128)(2,1)}, u32[]{:S(2)}, u32[]{:S(2)}) %collective-permute-start.2) | collective-permute-done | bytes 2359328 | tf_op jit(solution)/shard_map/ppermute | solution.py:17
  158.9 10.6 %maximum_maximum_fusion = (bf16[44,48,2048]{2,1,0:T(8,128)(2,1)S(1)}, bf16[44,48,2048]{2,1,0:T(8,128)(2,1)}) fusion(bf16[32,12,2048]{2,1,0:T(8,128)(2,1)S(1)} %copy-done.4, bf16[32,24,2048]{2,1,0:T(8,128)(2,1)S(1)} %copy-done.2, bf16[32,12,2048]{2,1,0:T(8,128)(2,1)S(1)} %copy-done.6, bf16[12,48,2048]{2,1,0:T(8,128)(2,1)} %collective-permute-done.2, ...), kind=kLoop, calls=%fused_computation.1 | loop fusion | flops 69206016 | bytes 28311552 | tf_op jit(solution)/shard_map/concatenate | solution.py:21
  169.5 10.5 %fusion.61 = (bf16[32,24,2048]{2,1,0:T(8,128)(2,1)}, bf16[32,24,2048]{2,1,0:T(8,128)(2,1)}, bf16[32,24,2048]{2,1,0:T(8,128)(2,1)}, bf16[32,24,2048]{2,1,0:T(8,12...) fusion(bf16[44,48,2048]{2,1,0:T(8,128)(2,1)S(1)} %get-tuple-element.24, ...), kind=kLoop, calls=%fused_computation.106 | loop fusion | bytes 37748736 | tf_op jit(solution)/shard_map/slice | solution.py:36
  180.0 3.3 fusion.30
  195.4 3.1 fusion.60
  198.5 70.8 %all-reduce.1 = (f32[256]{0:T(256)S(1)}, f32[256]{0:T(256)S(1)}) all-reduce(f32[256]{0:T(256)S(1)} %get-tuple-element.9, f32[256]{0:T(256)S(1)} %get-tuple-element.8), channel_id=1, replica_groups=mesh['lat'=8,'lon'=16] {'lat','lon'}, use_global_device_ids=true, to_apply=%region_3.0 | all-reduce | flops 512 | bytes 4096 | tf_op jit(solution)/shard_map/psum | solution.py:44
  271.9 3.0 fusion.59
  275.6 62.6 %all-reduce = (f32[]{:T(128)}, f32[256]{0:T(256)S(1)}, f32[256]{0:T(256)S(1)}, f32[3,256]{1,0:T(4,128)}) all-reduce(f32[]{:T(128)} %subtract_reduce_fusion, f32[256]{0:T(256)S(1)} %get-tuple-element.7, f32[256]{0:T(256)S(1)} %get-tuple-element.6, f32[3,256]{1,0:T(4,128)S(1)} %fusion.58), channel_id=1, replica_groups=mesh['lat'=8,'lon'=16] {'lat','lon'}, use_global_device_ids=true, to_apply=%region_7.8 | all-reduce | flops 1281 | bytes 10248 | tf_op jit(solution)/shard_map/psum | solution.py:64
  339.9 3.8 collective-permute-start.5
  343.7 6.5 %collective-permute-done.4 = bf16[32,12,256]{2,1,0:T(8,128)(2,1)S(1)} collective-permute-done((bf16[32,12,256]{2,1,0:T(8,128)(2,1)S(1)}, bf16[32,12,256]{2,1,0:T(8,128)(2,1)S(1)}, u32[]{:S(2)}, u32[]{:S(2)}) %collective-permute-start.4) | collective-permute-done | bytes 196640 | tf_op jit(solution)/shard_map/ppermute | solution.py:17
  351.7 6.1 %collective-permute-start.7 = (bf16[12,48,256]{2,1,0:T(8,128)(2,1)S(1)}, bf16[12,48,256]{2,1,0:T(8,128)(2,1)S(1)}, u32[]{:S(2)}, u32[]{:S(2)}) collective-permute-start(bf16[12,48,256]{2,1,0:T(8,128)(2,1)S(1)} %get-tuple-element.41), channel_id=1, source_target_pairs={{0,16},{16,32},{32,48},{48,64},{64,80},{80,96},{96,112},{1,17},{17... | collective-permute-start | bytes 884744 | tf_op jit(solution)/shard_map/ppermute | solution.py:17
  358.2 3.5 collective-permute-done.6
  361.7 4.8 collective-permute-done.7
  368.4 9.8 %convert_bitcast_fusion = bf16[256,9,2048]{2,0,1:T(8,128)(2,1)} fusion(bf16[9,768,256]{2,1,0:T(8,128)(2,1)S(1)} %bitcast_dynamic-update-slice_fusion, bf16[768,2048,1]{1,0,2:T(8,128)(2,1)S(1)} %bitcast.124), kind=kOutput, calls=%fused_computation | convolution fusion | flops 7252475904 | bytes 16121856 | tf_op jit(solution)/shard_map/tqf,qc->ftc/dot_general | solution.py:98
  379.8 5.1 fusion.20
  384.9 5.0 fusion.17
  389.9 3.7 fusion.24
  393.6 3.6 fusion.13
  397.2 3.6 fusion.9
  400.8 3.7 fusion.36
  404.5 3.6 fusion.28
  408.1 3.6 fusion.32
  411.8 75.0 %reduce-scatter.3.cloned.1.call-done = bf16[16,9,2048]{2,0,1:T(8,128)(2,1)} async-done(((bf16[256,9,2048]{2,0,1:T(8,128)(2,1)}), bf16[16,9,2048]{2,0,1:T(8,128)(2,1)}) %reduce-scatter.3.cloned.1.call-update) | async-done | bytes 589840 | tf_op jit(solution)/shard_map/reduce_scatter | solution.py:97
  486.8 18.9 %add_convert_fusion = bf16[768,2048]{1,0:T(8,128)(2,1)} fusion(f32[768,2048]{1,0:T(8,128)} %fusion.9, f32[768,2048]{1,0:T(8,128)} %fusion.13, f32[768,2048]{1,0:T(8,128)} %fusion.17, f32[768,2048]{1,0:T(8,128)} %fusion.20, f32[768,2048]{1,0:T(8,128)} %fusion.24, f32[768,2048]{1,0:T(8,128)} %fusion.28, f32[768,2048]{1,0:T(8,128)} %fusion.36, ...), kind=kOutput, calls=%fused_computation.3 | convolution fusion | flops 819462144 | bytes 54919168 | tf_op jit(solution)/shard_map/dot_general | solution.py:87
  505.7 51.4 %reduce-scatter.5.cloned.1.call-done = bf16[16,9,256]{2,0,1:T(8,128)(2,1)} async-done(((bf16[16,9,2048]{2,0,1:T(8,128)(2,1)}), bf16[16,9,256]{2,0,1:T(8,128)(2,1)}) %reduce-scatter.5.cloned.1.call-update) | async-done | bytes 73744 | tf_op jit(solution)/shard_map/reduce_scatter | solution.py:106
  (127 shorter events, 33.1 us)
Async XLA Ops:
  7.2 264.0 %copy-start = (f32[3,256]{1,0:T(4,128)S(1)}, f32[3,256]{1,0:T(4,128)}, u32[]{:S(2)}) copy-start(f32[3,256]{1,0:T(4,128)} %param.10) | copy-start | bytes 9220
  7.2 479.5 %reduce-scatter.3.cloned.1.call-start = ((), (), s32[]{:S(2)}) async-start(), calls=%async_computation.2 | async-start | bytes 10027008 | tf_op jit(solution)/shard_map/reduce_scatter | solution.py:97
  11.2 36.9 %collective-permute-start.1 = (bf16[32,12,2048]{2,0,1:T(8,128)(2,1)S(1)}, bf16[32,12,2048]{2,0,1:T(8,128)(2,1)S(1)}, u32[]{:S(2)}, u32[]{:S(2)}) collective-permute-start(bf16[32,12,2048]{2,0,1:T(8,128)(2,1)S(1)} %copy.25), channel_id=1, source_target_pairs={{1,0},{2,1},{3,2},{4,3},{5,4},{6,5},{7,6},{8,7},{9,8},{10,9},{11,1... | collective-permute-start | bytes 4718600 | tf_op jit(solution)/shard_map/ppermute | solution.py:20
  16.7 35.8 %copy-start.2 = (bf16[32,24,2048]{2,1,0:T(8,128)(2,1)S(1)}, bf16[32,24,2048]{2,1,0:T(8,128)(2,1)}, u32[]{:S(2)}) copy-start(bf16[32,24,2048]{2,1,0:T(8,128)(2,1)} %param.6) | copy-start | bytes 9437188
  16.7 34.9 %collective-permute-start = (bf16[32,12,2048]{2,0,1:T(8,128)(2,1)S(1)}, bf16[32,12,2048]{2,0,1:T(8,128)(2,1)S(1)}, u32[]{:S(2)}, u32[]{:S(2)}) collective-permute-start(bf16[32,12,2048]{2,0,1:T(8,128)(2,1)S(1)} %copy.24), channel_id=1, source_target_pairs={{0,1},{1,2},{2,3},{3,4},{4,5},{5,6},{6,7},{7,8},{8,9},{9,10},{10,1... | collective-permute-start | bytes 4718600 | tf_op jit(solution)/shard_map/ppermute | solution.py:17
  49.0 8.4 %copy-start.3 = (bf16[32,12,2048]{2,1,0:T(8,128)(2,1)}, bf16[32,12,2048]{2,1,0:T(8,128)(2,1)S(1)}, u32[]{:S(2)}) copy-start(bf16[32,12,2048]{2,1,0:T(8,128)(2,1)S(1)} %copy.18) | copy-start | bytes 4718596
  52.6 4.9 copy-start.5
  52.6 12.6 %copy-start.30 = (s32[32,24]{0,1:T(8,128)S(1)}, s32[32,24]{0,1:T(8,128)}, u32[]{:S(2)}) copy-start(s32[32,24]{0,1:T(8,128)} %param.11) | copy-start | bytes 9220
  57.4 101.4 %collective-permute-start.2 = (bf16[12,48,2048]{2,1,0:T(8,128)(2,1)}, bf16[12,48,2048]{2,1,0:T(8,128)(2,1)}, u32[]{:S(2)}, u32[]{:S(2)}) collective-permute-start(bf16[12,48,2048]{2,1,0:T(8,128)(2,1)} %get-tuple-element.26), channel_id=1, source_target_pairs={{0,16},{16,32},{32,48},{48,64},{64,80},{80,96},{96,112},{1,17},{17... | collective-permute-start | bytes 7077896 | tf_op jit(solution)/shard_map/ppermute | solution.py:17
  63.9 95.0 %collective-permute-start.3 = (bf16[12,48,2048]{2,1,0:T(8,128)(2,1)}, bf16[12,48,2048]{2,1,0:T(8,128)(2,1)}, u32[]{:S(2)}, u32[]{:S(2)}) collective-permute-start(bf16[12,48,2048]{2,1,0:T(8,128)(2,1)} %get-tuple-element.27), channel_id=1, source_target_pairs={{16,0},{32,16},{48,32},{64,48},{80,64},{96,80},{112,96},{17,1},{33... | collective-permute-start | bytes 7077896 | tf_op jit(solution)/shard_map/ppermute | solution.py:20
  195.4 73.9 %copy-start.33 = (f32[256]{0:T(256)S(1)}, f32[256]{0:T(256)}, u32[]{:S(2)}) copy-start(f32[256]{0:T(256)} %param.8) | copy-start | bytes 3076
  195.4 74.5 %copy-start.35 = (f32[256]{0:T(256)S(1)}, f32[256]{0:T(256)}, u32[]{:S(2)}) copy-start(f32[256]{0:T(256)} %param.9) | copy-start | bytes 3076
  338.1 28.7 %copy-start.31 = (f32[256]{0:T(256)}, f32[256]{0:T(256)S(1)}, u32[]{:S(2)}) copy-start(f32[256]{0:T(256)S(1)} %broadcast_multiply_fusion.1) | copy-start | bytes 3076
  338.1 28.7 %copy-start.32 = (f32[256]{0:T(256)}, f32[256]{0:T(256)S(1)}, u32[]{:S(2)}) copy-start(f32[256]{0:T(256)S(1)} %broadcast_multiply_fusion.2) | copy-start | bytes 3076
  339.8 10.4 %collective-permute-start.4 = (bf16[32,12,256]{2,1,0:T(8,128)(2,1)S(1)}, bf16[32,12,256]{2,1,0:T(8,128)(2,1)S(1)}, u32[]{:S(2)}, u32[]{:S(2)}) collective-permute-start(bf16[32,12,256]{2,1,0:T(8,128)(2,1)S(1)} %get-tuple-element.44), channel_id=1, source_target_pairs={{0,1},{1,2},{2,3},{3,4},{4,5},{5,6},{6,7},{7,8},{8,9},{9,10},{10,1... | collective-permute-start | bytes 589832 | tf_op jit(solution)/shard_map/ppermute | solution.py:17
  339.9 10.4 %collective-permute-start.5 = (bf16[32,12,256]{2,1,0:T(8,128)(2,1)S(1)}, bf16[32,12,256]{2,1,0:T(8,128)(2,1)S(1)}, u32[]{:S(2)}, u32[]{:S(2)}) collective-permute-start(bf16[32,12,256]{2,1,0:T(8,128)(2,1)S(1)} %get-tuple-element.45), channel_id=1, source_target_pairs={{1,0},{2,1},{3,2},{4,3},{5,4},{6,5},{7,6},{8,7},{9,8},{10,9},{11,1... | collective-permute-start | bytes 589832 | tf_op jit(solution)/shard_map/ppermute | solution.py:20
  350.4 11.2 %collective-permute-start.6 = (bf16[12,48,256]{2,1,0:T(8,128)(2,1)S(1)}, bf16[12,48,256]{2,1,0:T(8,128)(2,1)S(1)}, u32[]{:S(2)}, u32[]{:S(2)}) collective-permute-start(bf16[12,48,256]{2,1,0:T(8,128)(2,1)S(1)} %get-tuple-element.40), channel_id=1, source_target_pairs={{16,0},{32,16},{48,32},{64,48},{80,64},{96,80},{112,96},{17,1},{33... | collective-permute-start | bytes 884744 | tf_op jit(solution)/shard_map/ppermute | solution.py:20
  351.7 14.7 %collective-permute-start.7 = (bf16[12,48,256]{2,1,0:T(8,128)(2,1)S(1)}, bf16[12,48,256]{2,1,0:T(8,128)(2,1)S(1)}, u32[]{:S(2)}, u32[]{:S(2)}) collective-permute-start(bf16[12,48,256]{2,1,0:T(8,128)(2,1)S(1)} %get-tuple-element.41), channel_id=1, source_target_pairs={{0,16},{16,32},{32,48},{48,64},{64,80},{80,96},{96,112},{1,17},{17... | collective-permute-start | bytes 884744 | tf_op jit(solution)/shard_map/ppermute | solution.py:17
  358.1 9.3 %copy-start.19 = (bf16[32,24,256]{2,1,0:T(8,128)(2,1)}, bf16[32,24,256]{2,1,0:T(8,128)(2,1)S(1)}, u32[]{:S(2)}) copy-start(bf16[32,24,256]{2,1,0:T(8,128)(2,1)S(1)} %get-tuple-element.42) | copy-start | bytes 1179652
  358.1 9.4 %copy-start.21 = (bf16[32,24,256]{2,1,0:T(8,128)(2,1)}, bf16[32,24,256]{2,1,0:T(8,128)(2,1)S(1)}, u32[]{:S(2)}) copy-start(bf16[32,24,256]{2,1,0:T(8,128)(2,1)S(1)} %get-tuple-element.43) | copy-start | bytes 1179652
  378.3 178.7 %reduce-scatter.5.cloned.1.call-start = ((), (), s32[]{:S(2)}) async-start(), calls=%async_computation.3 | async-start | bytes 663552 | tf_op jit(solution)/shard_map/reduce_scatter | solution.py:106
  379.8 5.1 copy-start.22
  379.8 10.0 %slice-start = ((s8[9437184]{0:T(1024)(128)(4,1)}), s8[4194304]{0:T(1024)(128)(4,1)S(1)}, s32[]{:S(2)}) async-start(s8[9437184]{0:T(1024)(128)(4,1)} %bitcast.131), calls=%async_computation.4 | async-start | bytes 8388608
  379.8 10.0 %slice-start.1 = ((s8[9437184]{0:T(1024)(128)(4,1)}), s8[4194304]{0:T(1024)(128)(4,1)S(1)}, s32[]{:S(2)}) async-start(s8[9437184]{0:T(1024)(128)(4,1)} %bitcast.131), calls=%async_computation.5 | async-start | bytes 8388608
  384.9 5.0 slice-start.2
  384.9 5.0 copy-start.20
  389.9 3.7 copy-start.18
  397.2 3.6 copy-start.14
  400.8 3.7 copy-start.12
  404.5 3.6 copy-start.10
  408.1 78.6 %copy-start.24 = (bf16[32,24,256]{2,1,0:T(8,128)(2,1)S(1)}, bf16[32,24,256]{2,1,0:T(8,128)(2,1)}, u32[]{:S(2)}) copy-start(bf16[32,24,256]{2,1,0:T(8,128)(2,1)} %copy-done.23) | copy-start | bytes 1179652
  486.8 71.8 %copy-start.1 = (f32[3,256]{1,0:T(4,128)S(1)}, f32[3,256]{1,0:T(4,128)}, u32[]{:S(2)}) copy-start(f32[3,256]{1,0:T(4,128)} %param.10) | copy-start | bytes 9220
  (17 other events, 32.8 us)
Sparse Core Ops, SparseCore 0:
  378.4 108.2 reduce-scatter.2
  490.3 66.6 reduce-scatter.4
where the time goes:
time: 574 us; the launch traced here: 567 us
  waiting for transfers between devices  259 us (45%)
  blocking collectives  133 us (23%)
  matrix products  88.1 us (15%)
  other arithmetic  26.7 us (5%)
  starting transfers between devices  24 us (4%)
  local copies, waits for them, and re-layouts  19.1 us (3%)
  between operations  16.7 us (3%)
    ppermute x4, waiting for transfers between devices, padded_2(): lax.ppermute(lax.slice_in_dim(block, block.shape[dim] - width, None, axis...  97.7 us
    reduce_scatter x1, waiting for transfers between devices, shards(): lax.psum_scatter(jnp.einsum('tqf,qc->ftc', shifted_all, flat_input, prefe...  75 us
    psum x1, blocking collectives, shards(): lax.psum((jnp.sum(summed, 0), jnp.sum(summed * summed, 0)), ('lat', 'lon'))  70.8 us
    psum x1, blocking collectives, shards(): lax.psum((jnp.sum(d_preact, 0), jnp.sum(d_preact * normed, 0), head_term,...  62.6 us
    reduce_scatter x1, waiting for transfers between devices, shards(): lax.psum_scatter(lon_summed, 'lat', scatter_dimension=2, tiled=True)  51.4 us
    dot_general x9, matrix products, shards(): lax.dot_general(shifted, atrous_weight[tap_row, tap_col], (((1,), (1,)),...  50.8 us
    ppermute x4, waiting for transfers between devices, padded_2(): lax.ppermute(lax.slice_in_dim(block, 0, width, axis=dim), axis, backward)  34.8 us
    dot_general x9, matrix products, shards(): jnp.dot(window.reshape(local_cells, channels), atrous_weight[tap_row, tap...  23.8 us
  transfers between devices with their start and end apart: 10, of which 8 were waited for; matrix products, arithmetic and copies ran while one was open for 11% of the time, Pallas kernels for 0%

commit v1 on v0

--- a/solution.py
+++ b/solution.py
@@ -41,7 +41,7 @@
                 atrous_weight[tap_row, tap_col],
                 preferred_element_type=jnp.float32,
             )
-    moments = lax.psum((jnp.sum(summed, 0), jnp.sum(summed * summed, 0)), ("lat", "lon"))
+    moments = lax.psum(lax.psum((jnp.sum(summed, 0), jnp.sum(summed * summed, 0)), "lat"), "lon")
     average = moments[0] / total_cells
     variance = moments[1] / total_cells - average * average
     inverse = lax.rsqrt(variance + epsilon)

time: 574 us -> 555 us (0.967)
  blocking collectives: 133 us -> 115 us
    psum x1 -> x2, blocking collectives: 70.8 us -> 52.7 us  [the longest x1 29.4 us: shards(): lax.psum(lax.psum((jnp.sum(summed, 0), jnp.sum(summed * summed, 0)), 'lat...]
  transfers between devices with their start and end apart: 10 -> 10, of which waited for: 8 -> 8; matrix products, arithmetic and copies ran while one was open for 11% -> 12% of each run, Pallas kernels for 0% -> 0%
where the time goes in v1:
time: 555 us; the launch traced here: 549 us
  waiting for transfers between devices  259 us (47%)
  blocking collectives  115 us (21%)
  matrix products  88.2 us (16%)
  other arithmetic  26.7 us (5%)
  starting transfers between devices  24 us (4%)
  local copies, waits for them, and re-layouts  19.2 us (3%)
  between operations  16.7 us (3%)
    ppermute x4, waiting for transfers between devices, padded_2(): lax.ppermute(lax.slice_in_dim(block, block.shape[dim] - width, None, axis...  97.7 us
    reduce_scatter x1, waiting for transfers between devices, shards(): lax.psum_scatter(jnp.einsum('tqf,qc->ftc', shifted_all, flat_input, prefe...  74.3 us
    psum x1, blocking collectives, shards(): lax.psum((jnp.sum(d_preact, 0), jnp.sum(d_preact * normed, 0), head_term,...  62.4 us
    reduce_scatter x1, waiting for transfers between devices, shards(): lax.psum_scatter(lon_summed, 'lat', scatter_dimension=2, tiled=True)  51.4 us
    dot_general x9, matrix products, shards(): lax.dot_general(shifted, atrous_weight[tap_row, tap_col], (((1,), (1,)),...  50.8 us
    ppermute x4, waiting for transfers between devices, padded_2(): lax.ppermute(lax.slice_in_dim(block, 0, width, axis=dim), axis, backward)  35.3 us
    psum x1, blocking collectives, shards(): lax.psum(lax.psum((jnp.sum(summed, 0), jnp.sum(summed * summed, 0)), 'lat...  29.4 us
    dot_general x9, matrix products, shards(): jnp.dot(window.reshape(local_cells, channels), atrous_weight[tap_row, tap...  23.8 us
  transfers between devices with their start and end apart: 10, of which 8 were waited for; matrix products, arithmetic and copies ran while one was open for 12% of the time, Pallas kernels for 0%

profile of v1, /device:TPU:0, one launch (start us, length us, event | category | flops | bytes accessed | tf_op | source)
XLA Modules:
  0.0 548.6 jit_solution(12151367167659939716)
XLA Ops:
  7.2 3.1 fusion.63
  11.2 4.6 collective-permute-start.1
  16.8 31.3 %collective-permute-done.1 = bf16[32,12,2048]{2,0,1:T(8,128)(2,1)S(1)} collective-permute-done((bf16[32,12,2048]{2,0,1:T(8,128)(2,1)S(1)}, bf16[32,12,2048]{2,0,1:T(8,128)(2,1)S(1)}, u32[]{:S(2)}, u32[]{:S(2)}) %collective-permute-start.1) | collective-permute-done | bytes 1572896 | tf_op jit(solution)/shard_map/ppermute | solution.py:20
  52.6 4.8 pad_maximum_fusion.5
  57.4 6.4 %collective-permute-start.2 = (bf16[12,48,2048]{2,1,0:T(8,128)(2,1)}, bf16[12,48,2048]{2,1,0:T(8,128)(2,1)}, u32[]{:S(2)}, u32[]{:S(2)}) collective-permute-start(bf16[12,48,2048]{2,1,0:T(8,128)(2,1)} %get-tuple-element.28), channel_id=1, source_target_pairs={{0,16},{16,32},{32,48},{48,64},{64,80},{80,96},{96,112},{1,17},{17... | collective-permute-start | bytes 7077896 | tf_op jit(solution)/shard_map/ppermute | solution.py:17
  67.9 4.2 pad_maximum_fusion.1
  72.0 3.1 fusion.26
  75.1 83.8 %collective-permute-done.2 = bf16[12,48,2048]{2,1,0:T(8,128)(2,1)} collective-permute-done((bf16[12,48,2048]{2,1,0:T(8,128)(2,1)}, bf16[12,48,2048]{2,1,0:T(8,128)(2,1)}, u32[]{:S(2)}, u32[]{:S(2)}) %collective-permute-start.2) | collective-permute-done | bytes 2359328 | tf_op jit(solution)/shard_map/ppermute | solution.py:17
  158.9 10.6 %maximum_maximum_fusion = (bf16[44,48,2048]{2,1,0:T(8,128)(2,1)S(1)}, bf16[44,48,2048]{2,1,0:T(8,128)(2,1)}) fusion(bf16[32,12,2048]{2,1,0:T(8,128)(2,1)S(1)} %copy-done.4, bf16[32,24,2048]{2,1,0:T(8,128)(2,1)S(1)} %copy-done.2, bf16[32,12,2048]{2,1,0:T(8,128)(2,1)S(1)} %copy-done.6, bf16[12,48,2048]{2,1,0:T(8,128)(2,1)} %collective-permute-done.2, ...), kind=kLoop, calls=%fused_computation.1 | loop fusion | flops 69206016 | bytes 28311552 | tf_op jit(solution)/shard_map/concatenate | solution.py:21
  169.5 10.6 %fusion.61 = (bf16[32,24,2048]{2,1,0:T(8,128)(2,1)}, bf16[32,24,2048]{2,1,0:T(8,128)(2,1)}, bf16[32,24,2048]{2,1,0:T(8,128)(2,1)}, bf16[32,24,2048]{2,1,0:T(8,12...) fusion(bf16[44,48,2048]{2,1,0:T(8,128)(2,1)S(1)} %get-tuple-element.26, ...), kind=kLoop, calls=%fused_computation.106 | loop fusion | bytes 37748736 | tf_op jit(solution)/shard_map/slice | solution.py:36
  180.1 3.3 fusion.30
  195.5 3.1 fusion.60
  198.6 23.3 %all-reduce.2 = (f32[256]{0:T(256)S(1)}, f32[256]{0:T(256)S(1)}) all-reduce(f32[256]{0:T(256)S(1)} %get-tuple-element.9, f32[256]{0:T(256)S(1)} %get-tuple-element.8), channel_id=1, replica_groups=mesh['lat'=8,'lon'=16] {'lat'}, use_global_device_ids=true, to_apply=%region_4.0 | all-reduce | flops 512 | bytes 4096 | tf_op jit(solution)/shard_map/psum | solution.py:44
  221.9 29.4 %all-reduce.1 = (f32[256]{0:T(256)S(1)}, f32[256]{0:T(256)S(1)}) all-reduce(f32[256]{0:T(256)S(1)} %get-tuple-element.18, f32[256]{0:T(256)S(1)} %get-tuple-element.19), channel_id=1, replica_groups=mesh['lat'=8,'lon'=16] {'lon'}, use_global_device_ids=true, to_apply=%region_5.0 | all-reduce | flops 512 | bytes 4096 | tf_op jit(solution)/shard_map/psum | solution.py:44
  257.6 62.4 %all-reduce = (f32[]{:T(128)}, f32[256]{0:T(256)S(1)}, f32[256]{0:T(256)S(1)}, f32[3,256]{1,0:T(4,128)}) all-reduce(f32[]{:T(128)} %subtract_reduce_fusion, f32[256]{0:T(256)S(1)} %get-tuple-element.7, f32[256]{0:T(256)S(1)} %get-tuple-element.6, f32[3,256]{1,0:T(4,128)S(1)} %fusion.58), channel_id=1, replica_groups=mesh['lat'=8,'lon'=16] {'lat','lon'}, use_global_device_ids=true, to_apply=%region_9.10 | all-reduce | flops 1281 | bytes 10248 | tf_op jit(solution)/shard_map/psum | solution.py:64
  321.8 3.8 collective-permute-start.5
  325.7 6.7 %collective-permute-done.4 = bf16[32,12,256]{2,1,0:T(8,128)(2,1)S(1)} collective-permute-done((bf16[32,12,256]{2,1,0:T(8,128)(2,1)S(1)}, bf16[32,12,256]{2,1,0:T(8,128)(2,1)S(1)}, u32[]{:S(2)}, u32[]{:S(2)}) %collective-permute-start.4) | collective-permute-done | bytes 196640 | tf_op jit(solution)/shard_map/ppermute | solution.py:17
  333.8 6.1 %collective-permute-start.7 = (bf16[12,48,256]{2,1,0:T(8,128)(2,1)S(1)}, bf16[12,48,256]{2,1,0:T(8,128)(2,1)S(1)}, u32[]{:S(2)}, u32[]{:S(2)}) collective-permute-start(bf16[12,48,256]{2,1,0:T(8,128)(2,1)S(1)} %get-tuple-element.43), channel_id=1, source_target_pairs={{0,16},{16,32},{32,48},{48,64},{64,80},{80,96},{96,112},{1,17},{17... | collective-permute-start | bytes 884744 | tf_op jit(solution)/shard_map/ppermute | solution.py:17
  340.2 4.0 collective-permute-done.6
  344.2 4.6 collective-permute-done.7
  350.8 9.8 %convert_bitcast_fusion = bf16[256,9,2048]{2,0,1:T(8,128)(2,1)} fusion(bf16[9,768,256]{2,1,0:T(8,128)(2,1)S(1)} %bitcast_dynamic-update-slice_fusion, bf16[768,2048,1]{1,0,2:T(8,128)(2,1)S(1)} %bitcast.124), kind=kOutput, calls=%fused_computation | convolution fusion | flops 7252475904 | bytes 16121856 | tf_op jit(solution)/shard_map/tqf,qc->ftc/dot_general | solution.py:98
  362.2 5.1 fusion.20
  367.2 5.0 fusion.17
  372.3 3.7 fusion.24
  376.0 3.6 fusion.13
  379.6 3.6 fusion.9
  383.2 3.7 fusion.36
  386.9 3.6 fusion.28
  390.6 3.6 fusion.32
  394.2 74.3 %reduce-scatter.3.cloned.1.call-done = bf16[16,9,2048]{2,0,1:T(8,128)(2,1)} async-done(((bf16[256,9,2048]{2,0,1:T(8,128)(2,1)}), bf16[16,9,2048]{2,0,1:T(8,128)(2,1)}) %reduce-scatter.3.cloned.1.call-update) | async-done | bytes 589840 | tf_op jit(solution)/shard_map/reduce_scatter | solution.py:97
  468.6 18.9 %add_convert_fusion = bf16[768,2048]{1,0:T(8,128)(2,1)} fusion(f32[768,2048]{1,0:T(8,128)} %fusion.9, f32[768,2048]{1,0:T(8,128)} %fusion.13, f32[768,2048]{1,0:T(8,128)} %fusion.17, f32[768,2048]{1,0:T(8,128)} %fusion.20, f32[768,2048]{1,0:T(8,128)} %fusion.24, f32[768,2048]{1,0:T(8,128)} %fusion.28, f32[768,2048]{1,0:T(8,128)} %fusion.36, ...), kind=kOutput, calls=%fused_computation.3 | convolution fusion | flops 819462144 | bytes 54919168 | tf_op jit(solution)/shard_map/dot_general | solution.py:87
  487.5 51.4 %reduce-scatter.5.cloned.1.call-done = bf16[16,9,256]{2,0,1:T(8,128)(2,1)} async-done(((bf16[16,9,2048]{2,0,1:T(8,128)(2,1)}), bf16[16,9,256]{2,0,1:T(8,128)(2,1)}) %reduce-scatter.5.cloned.1.call-update) | async-done | bytes 73744 | tf_op jit(solution)/shard_map/reduce_scatter | solution.py:106
  (128 shorter events, 36.2 us)
Async XLA Ops:
  7.2 246.0 %copy-start = (f32[3,256]{1,0:T(4,128)S(1)}, f32[3,256]{1,0:T(4,128)}, u32[]{:S(2)}) copy-start(f32[3,256]{1,0:T(4,128)} %param.10) | copy-start | bytes 9220
  7.2 461.3 %reduce-scatter.3.cloned.1.call-start = ((), (), s32[]{:S(2)}) async-start(), calls=%async_computation.2 | async-start | bytes 10027008 | tf_op jit(solution)/shard_map/reduce_scatter | solution.py:97
  11.2 36.9 %collective-permute-start.1 = (bf16[32,12,2048]{2,0,1:T(8,128)(2,1)S(1)}, bf16[32,12,2048]{2,0,1:T(8,128)(2,1)S(1)}, u32[]{:S(2)}, u32[]{:S(2)}) collective-permute-start(bf16[32,12,2048]{2,0,1:T(8,128)(2,1)S(1)} %copy.25), channel_id=1, source_target_pairs={{1,0},{2,1},{3,2},{4,3},{5,4},{6,5},{7,6},{8,7},{9,8},{10,9},{11,1... | collective-permute-start | bytes 4718600 | tf_op jit(solution)/shard_map/ppermute | solution.py:20
  16.7 35.8 %copy-start.2 = (bf16[32,24,2048]{2,1,0:T(8,128)(2,1)S(1)}, bf16[32,24,2048]{2,1,0:T(8,128)(2,1)}, u32[]{:S(2)}) copy-start(bf16[32,24,2048]{2,1,0:T(8,128)(2,1)} %param.6) | copy-start | bytes 9437188
  16.7 34.9 %collective-permute-start = (bf16[32,12,2048]{2,0,1:T(8,128)(2,1)S(1)}, bf16[32,12,2048]{2,0,1:T(8,128)(2,1)S(1)}, u32[]{:S(2)}, u32[]{:S(2)}) collective-permute-start(bf16[32,12,2048]{2,0,1:T(8,128)(2,1)S(1)} %copy.24), channel_id=1, source_target_pairs={{0,1},{1,2},{2,3},{3,4},{4,5},{5,6},{6,7},{7,8},{8,9},{9,10},{10,1... | collective-permute-start | bytes 4718600 | tf_op jit(solution)/shard_map/ppermute | solution.py:17
  49.0 8.4 %copy-start.3 = (bf16[32,12,2048]{2,1,0:T(8,128)(2,1)}, bf16[32,12,2048]{2,1,0:T(8,128)(2,1)S(1)}, u32[]{:S(2)}) copy-start(bf16[32,12,2048]{2,1,0:T(8,128)(2,1)S(1)} %copy.18) | copy-start | bytes 4718596
  52.6 4.9 copy-start.5
  52.6 12.6 %copy-start.30 = (s32[32,24]{0,1:T(8,128)S(1)}, s32[32,24]{0,1:T(8,128)}, u32[]{:S(2)}) copy-start(s32[32,24]{0,1:T(8,128)} %param.11) | copy-start | bytes 9220
  57.4 101.4 %collective-permute-start.2 = (bf16[12,48,2048]{2,1,0:T(8,128)(2,1)}, bf16[12,48,2048]{2,1,0:T(8,128)(2,1)}, u32[]{:S(2)}, u32[]{:S(2)}) collective-permute-start(bf16[12,48,2048]{2,1,0:T(8,128)(2,1)} %get-tuple-element.28), channel_id=1, source_target_pairs={{0,16},{16,32},{32,48},{48,64},{64,80},{80,96},{96,112},{1,17},{17... | collective-permute-start | bytes 7077896 | tf_op jit(solution)/shard_map/ppermute | solution.py:17
  63.9 95.0 %collective-permute-start.3 = (bf16[12,48,2048]{2,1,0:T(8,128)(2,1)}, bf16[12,48,2048]{2,1,0:T(8,128)(2,1)}, u32[]{:S(2)}, u32[]{:S(2)}) collective-permute-start(bf16[12,48,2048]{2,1,0:T(8,128)(2,1)} %get-tuple-element.29), channel_id=1, source_target_pairs={{16,0},{32,16},{48,32},{64,48},{80,64},{96,80},{112,96},{17,1},{33... | collective-permute-start | bytes 7077896 | tf_op jit(solution)/shard_map/ppermute | solution.py:20
  195.5 55.9 %copy-start.33 = (f32[256]{0:T(256)S(1)}, f32[256]{0:T(256)}, u32[]{:S(2)}) copy-start(f32[256]{0:T(256)} %param.8) | copy-start | bytes 3076
  195.5 56.4 %copy-start.35 = (f32[256]{0:T(256)S(1)}, f32[256]{0:T(256)}, u32[]{:S(2)}) copy-start(f32[256]{0:T(256)} %param.9) | copy-start | bytes 3076
  320.0 29.1 %copy-start.31 = (f32[256]{0:T(256)}, f32[256]{0:T(256)S(1)}, u32[]{:S(2)}) copy-start(f32[256]{0:T(256)S(1)} %broadcast_multiply_fusion.1) | copy-start | bytes 3076
  320.1 29.1 %copy-start.32 = (f32[256]{0:T(256)}, f32[256]{0:T(256)S(1)}, u32[]{:S(2)}) copy-start(f32[256]{0:T(256)S(1)} %broadcast_multiply_fusion.2) | copy-start | bytes 3076
  321.7 10.6 %collective-permute-start.4 = (bf16[32,12,256]{2,1,0:T(8,128)(2,1)S(1)}, bf16[32,12,256]{2,1,0:T(8,128)(2,1)S(1)}, u32[]{:S(2)}, u32[]{:S(2)}) collective-permute-start(bf16[32,12,256]{2,1,0:T(8,128)(2,1)S(1)} %get-tuple-element.46), channel_id=1, source_target_pairs={{0,1},{1,2},{2,3},{3,4},{4,5},{5,6},{6,7},{7,8},{8,9},{9,10},{10,1... | collective-permute-start | bytes 589832 | tf_op jit(solution)/shard_map/ppermute | solution.py:17
  321.8 10.5 %collective-permute-start.5 = (bf16[32,12,256]{2,1,0:T(8,128)(2,1)S(1)}, bf16[32,12,256]{2,1,0:T(8,128)(2,1)S(1)}, u32[]{:S(2)}, u32[]{:S(2)}) collective-permute-start(bf16[32,12,256]{2,1,0:T(8,128)(2,1)S(1)} %get-tuple-element.47), channel_id=1, source_target_pairs={{1,0},{2,1},{3,2},{4,3},{5,4},{6,5},{7,6},{8,7},{9,8},{10,9},{11,1... | collective-permute-start | bytes 589832 | tf_op jit(solution)/shard_map/ppermute | solution.py:20
  332.5 11.7 %collective-permute-start.6 = (bf16[12,48,256]{2,1,0:T(8,128)(2,1)S(1)}, bf16[12,48,256]{2,1,0:T(8,128)(2,1)S(1)}, u32[]{:S(2)}, u32[]{:S(2)}) collective-permute-start(bf16[12,48,256]{2,1,0:T(8,128)(2,1)S(1)} %get-tuple-element.42), channel_id=1, source_target_pairs={{16,0},{32,16},{48,32},{64,48},{80,64},{96,80},{112,96},{17,1},{33... | collective-permute-start | bytes 884744 | tf_op jit(solution)/shard_map/ppermute | solution.py:20
  333.8 15.0 %collective-permute-start.7 = (bf16[12,48,256]{2,1,0:T(8,128)(2,1)S(1)}, bf16[12,48,256]{2,1,0:T(8,128)(2,1)S(1)}, u32[]{:S(2)}, u32[]{:S(2)}) collective-permute-start(bf16[12,48,256]{2,1,0:T(8,128)(2,1)S(1)} %get-tuple-element.43), channel_id=1, source_target_pairs={{0,16},{16,32},{32,48},{48,64},{64,80},{80,96},{96,112},{1,17},{17... | collective-permute-start | bytes 884744 | tf_op jit(solution)/shard_map/ppermute | solution.py:17
  340.2 9.5 %copy-start.19 = (bf16[32,24,256]{2,1,0:T(8,128)(2,1)}, bf16[32,24,256]{2,1,0:T(8,128)(2,1)S(1)}, u32[]{:S(2)}) copy-start(bf16[32,24,256]{2,1,0:T(8,128)(2,1)S(1)} %get-tuple-element.44) | copy-start | bytes 1179652
  340.2 9.6 %copy-start.21 = (bf16[32,24,256]{2,1,0:T(8,128)(2,1)}, bf16[32,24,256]{2,1,0:T(8,128)(2,1)S(1)}, u32[]{:S(2)}) copy-start(bf16[32,24,256]{2,1,0:T(8,128)(2,1)S(1)} %get-tuple-element.45) | copy-start | bytes 1179652
  360.6 178.2 %reduce-scatter.5.cloned.1.call-start = ((), (), s32[]{:S(2)}) async-start(), calls=%async_computation.3 | async-start | bytes 663552 | tf_op jit(solution)/shard_map/reduce_scatter | solution.py:106
  362.1 5.1 copy-start.22
  362.1 10.1 %slice-start = ((s8[9437184]{0:T(1024)(128)(4,1)}), s8[4194304]{0:T(1024)(128)(4,1)S(1)}, s32[]{:S(2)}) async-start(s8[9437184]{0:T(1024)(128)(4,1)} %bitcast.131), calls=%async_computation.4 | async-start | bytes 8388608
  362.2 10.1 %slice-start.1 = ((s8[9437184]{0:T(1024)(128)(4,1)}), s8[4194304]{0:T(1024)(128)(4,1)S(1)}, s32[]{:S(2)}) async-start(s8[9437184]{0:T(1024)(128)(4,1)} %bitcast.131), calls=%async_computation.5 | async-start | bytes 8388608
  367.2 5.0 slice-start.2
  367.2 5.0 copy-start.20
  372.3 3.7 copy-start.18
  379.6 3.6 copy-start.14
  383.2 3.7 copy-start.12
  386.9 3.6 copy-start.10
  390.6 78.0 %copy-start.24 = (bf16[32,24,256]{2,1,0:T(8,128)(2,1)S(1)}, bf16[32,24,256]{2,1,0:T(8,128)(2,1)}, u32[]{:S(2)}) copy-start(bf16[32,24,256]{2,1,0:T(8,128)(2,1)} %copy-done.23) | copy-start | bytes 1179652
  468.6 71.8 %copy-start.1 = (f32[3,256]{1,0:T(4,128)S(1)}, f32[3,256]{1,0:T(4,128)}, u32[]{:S(2)}) copy-start(f32[3,256]{1,0:T(4,128)} %param.10) | copy-start | bytes 9220
  (17 other events, 32.9 us)
Sparse Core Ops, SparseCore 0:
  360.8 107.7 reduce-scatter.2
  472.1 66.6 reduce-scatter.4
